TPU v7x, 512 devices: a whole 4x8x8 slice. The times are simulated.
512 devices in a mesh: box: 32 (over x, y), dir: 16 (over z, core).
Axes of the slice: x: 4, y: 8, z: 8, core: 2. Of those that a mesh axis runs over, the one named last changes fastest.
Arguments:
- currents: bfloat16 [8192, 8, 128], P(('box', 'dir')), may hold values from -6 to 6
- positions: bfloat16 [8192, 3, 128], P(('box', 'dir')), may hold values from -2 to 2
- radiation: bfloat16 [128, 256], replicated, may hold values from -0.5 to 0.5
- interp_index: int32 [512, 4], replicated, may hold values from 0 to 127
- interp_weight: float32 [512, 4], replicated, may hold values from -3 to 3
- child_phase: float32 [8, 512], replicated, may hold values from -3.140625 to 3.140625
- near_src: int32 [8192, 27], P(('box', 'dir')), may hold values from 0 to 8191, as said below
- trans_src: int32 [1024, 32], P('box'), may hold values from 0 to 1023, as said below
- trans_id: int32 [1024, 32], P('box'), may hold values from 0 to 315
- trans_count: int32 [1024], P('box'), may hold values from 16 to 32, as said below
- trans_table: float32 [316, 2, 512], replicated, may hold values from -0.009 to 0.009
Outputs:
- field: float32 [8192, 8, 128], P(('box', 'dir'))
Inputs may be any that keep to these rules, and one draw needn't show every extreme that they name: `near_src`: entry 0 of row i is i itself; every entry lies in the block of 16 boxes that holds i or in a block beside it. `trans_src`: every entry lies in the block of 32 parents that holds the row's parent or in a block beside it. Entries at and after trans_count are ignored; some parent in every block of 32 has 32.
All inputs are finite; a program needn't handle non-finite values.
Results may differ from a plain program's by a relative error of at most 0.0045.
Values may be sent and summed in bfloat16 or wider, within the bound.
A program may use at most 64 MiB of HBM per device.

v0:
```python
import math

import jax
import jax.numpy as jnp
from jax import lax
from jax.sharding import PartitionSpec as P


def extended(x, sides, width):
    for axis, dim in sides:
        size, length = (lax.axis_size(axis), x.shape[dim])
        up = [(i, (i + 1) % size) for i in range(size - 1)]
        down = [(j, i) for i, j in up]
        last = lax.slice_in_dim(x, length - width, length, axis=dim)
        first = lax.slice_in_dim(x, 0, width, axis=dim)
        before = lax.ppermute(last, axis, up)
        after = lax.ppermute(first, axis, down)
        x = jnp.concatenate([before, x, after], axis=dim)
    return x


def interp_matrix(interp_index, interp_weight, leaf_dirs):
    columns = jnp.arange(leaf_dirs, dtype=jnp.int32)
    matches = (interp_index[:, :, None] == columns[None, None, :]).astype(jnp.float32)
    return jnp.sum(interp_weight[:, :, None] * matches, axis=1).T


def near_tiles(own_pos, src_pos):
    entries = src_pos.shape[1]
    width = src_pos.shape[3]
    dist_sq = jnp.zeros((own_pos.shape[0], entries, width, width), jnp.float32)
    for axis_num in range(3):
        offset = own_pos[:, None, axis_num, :, None] - src_pos[:, :, axis_num, None, :]
        dist_sq = dist_sq + offset * offset
    distance = jnp.sqrt(dist_sq)
    factor = 1.0 / math.sqrt(entries * width)
    return (jnp.cos(4.0 * distance) / (distance + 0.5) * factor).astype(jnp.bfloat16)


def translate(window, sources, list_ids, counts, trans_tab):
    spectra = window[sources].astype(jnp.float32)
    coeff = trans_tab[list_ids]
    entries = jnp.arange(sources.shape[1], dtype=jnp.int32)
    live_mask = (entries[None, :] < counts[:, None]).astype(jnp.float32)
    coeff_re = coeff[:, :, 0, None, :] * live_mask[:, :, None, None]
    coeff_im = coeff[:, :, 1, None, :] * live_mask[:, :, None, None]
    real_part = jnp.sum(coeff_re * spectra[:, :, 0] - coeff_im * spectra[:, :, 1], axis=1)
    imag_part = jnp.sum(coeff_re * spectra[:, :, 1] + coeff_im * spectra[:, :, 0], axis=1)
    return jnp.stack([real_part, imag_part], axis=1)


def per_device(
    currents,
    positions,
    radiation,
    interp_index,
    interp_weight,
    child_phase,
    near_src,
    trans_src,
    trans_id,
    trans_count,
    trans_table,
):
    boxes_here, waves, width = currents.shape
    entries = near_src.shape[1]
    leaf_dirs = radiation.shape[1] // 2
    parent_dirs = child_phase.shape[1]
    device_idx = lax.axis_index(("box", "dir"))
    joined = jnp.concatenate([currents, positions], axis=1)
    window = extended(joined, ((("box", "dir"), 0),), boxes_here)
    win_x = window[:, :waves]
    win_pos = window[:, waves:]
    near_local = near_src - (device_idx - 1) * boxes_here

    def near_block(packed):
        own_pos, src_ids = packed
        src_pos = win_pos[src_ids].astype(jnp.float32)
        src_x = win_x[src_ids]
        tiles = near_tiles(own_pos.astype(jnp.float32), src_pos)
        return jnp.einsum("bemn,bewn->bwm", tiles, src_x, preferred_element_type=jnp.float32)

    near_field = lax.map(
        near_block, (positions.reshape(-1, 8, 3, width), near_local.reshape(-1, 8, entries))
    )
    near_field = near_field.reshape(boxes_here, waves, width)
    parents_here = boxes_here // 8
    imatrix = interp_matrix(interp_index, interp_weight, leaf_dirs).astype(jnp.bfloat16)
    leaf = jnp.dot(
        currents.reshape(boxes_here * waves, width), radiation, preferred_element_type=jnp.float32
    ).astype(jnp.bfloat16)
    up_re = jnp.dot(leaf[:, :leaf_dirs], imatrix, preferred_element_type=jnp.float32).reshape(
        parents_here, 8, waves, parent_dirs
    )
    up_im = jnp.dot(leaf[:, leaf_dirs:], imatrix, preferred_element_type=jnp.float32).reshape(
        parents_here, 8, waves, parent_dirs
    )
    cos_phase = jnp.cos(child_phase)[None, :, None, :]
    sin_phase = jnp.sin(child_phase)[None, :, None, :]
    parent_re = jnp.sum(cos_phase * up_re - sin_phase * up_im, axis=1)
    parent_im = jnp.sum(sin_phase * up_re + cos_phase * up_im, axis=1)
    parent = jnp.stack([parent_re, parent_im], axis=1).astype(jnp.bfloat16)
    dir_count = lax.axis_size("dir")
    group_rows = parents_here * dir_count
    box_idx = lax.axis_index("box")
    dir_idx = lax.axis_index("dir")
    group_spec = lax.all_gather(parent, "dir", axis=0, tiled=True)
    window_par = extended(group_spec, (("box", 0),), group_rows)
    own_src = (
        lax.dynamic_slice_in_dim(trans_src, dir_idx * parents_here, parents_here, 0)
        - (box_idx - 1) * group_rows
    )
    own_ids = lax.dynamic_slice_in_dim(trans_id, dir_idx * parents_here, parents_here, 0)
    own_counts = lax.dynamic_slice_in_dim(trans_count, dir_idx * parents_here, parents_here, 0)
    local_field = translate(window_par, own_src, own_ids, own_counts, trans_table).astype(
        jnp.bfloat16
    )
    local_field = lax.optimization_barrier(local_field)
    local_field = local_field.astype(jnp.float32)
    loc_re = local_field[:, 0][:, None]
    loc_im = local_field[:, 1][:, None]
    down_re = (
        (cos_phase * loc_re + sin_phase * loc_im)
        .reshape(boxes_here * waves, parent_dirs)
        .astype(jnp.bfloat16)
    )
    down_im = (
        (cos_phase * loc_im - sin_phase * loc_re)
        .reshape(boxes_here * waves, parent_dirs)
        .astype(jnp.bfloat16)
    )
    in_re = jnp.dot(down_re, imatrix.T, preferred_element_type=jnp.float32)
    in_im = jnp.dot(down_im, imatrix.T, preferred_element_type=jnp.float32)
    incoming = jnp.concatenate([in_re, in_im], axis=1).astype(jnp.bfloat16)
    far_field = lax.dot_general(
        incoming, radiation, (((1,), (1,)), ((), ())), preferred_element_type=jnp.float32
    )
    return near_field + far_field.reshape(boxes_here, waves, width)


def solution(mesh):
    placed = (
        P(("box", "dir"), None, None),
        P(("box", "dir"), None, None),
        P(),
        P(),
        P(),
        P(),
        P(("box", "dir"), None),
        P("box", None),
        P("box", None),
        P("box"),
        P(),
    )
    return jax.shard_map(
        per_device,
        mesh=mesh,
        in_specs=placed,
        out_specs=P(("box", "dir"), None, None),
        check_vma=False,
    )
```

profile of v0, /device:TPU:4, one launch (start us, length us, event | category | flops | bytes accessed | tf_op | source)
XLA Modules:
  0.0 189.4 jit_solution(1456497982869118861)
XLA Ops:
  0.0 1.5 select_reduce_fusion
  1.5 1.0 convolution_convert_fusion
  2.5 0.2 fusion.12
  2.7 0.2 fusion.10
  2.9 0.8 fusion.16
  3.7 0.1 subtract_reduce_fusion.1
  3.8 24.6 %all_gather.3 = bf16[32,2,8,512]{3,2,1,0:T(8,128)(2,1)S(1)} all-gather(bf16[2,2,8,512]{3,2,1,0:T(8,128)(2,1)S(1)} %pad_maximum_fusion.3), channel_id=1, replica_groups=mesh['box'=32,'dir'=16] {'dir'}, dimensions={0}, use_global_device_ids=true | all-gather | bytes 557056 | tf_op jit(solution)/shard_map/all_gather | solution.py:107
  28.4 3.5 %collective-permute-start.2 = (bf16[32,2,8,512]{3,2,1,0:T(8,128)(2,1)S(1)}, bf16[32,2,8,512]{3,2,1,0:T(8,128)(2,1)S(1)}, u32[]{:S(2)}, u32[]{:S(2)}) collective-permute-start(bf16[32,2,8,512]{3,2,1,0:T(8,128)(2,1)S(1)} %all_gather.3), channel_id=1, source_target_pairs={{0,16},{16,32},{32,48},{48,64},{64,80},{80,96},{96,112},{112,128},... | collective-permute-start | bytes 1572872 | tf_op jit(solution)/shard_map/ppermute | solution.py:16
  31.9 4.5 %collective-permute-start.3 = (bf16[32,2,8,512]{3,2,1,0:T(8,128)(2,1)S(1)}, bf16[32,2,8,512]{3,2,1,0:T(8,128)(2,1)}, u32[]{:S(2)}, u32[]{:S(2)}) collective-permute-start(bf16[32,2,8,512]{3,2,1,0:T(8,128)(2,1)S(1)} %all_gather.3), channel_id=1, source_target_pairs={{16,0},{32,16},{48,32},{64,48},{80,64},{96,80},{112,96},{128,112},... | collective-permute-start | bytes 1572872 | tf_op jit(solution)/shard_map/ppermute | solution.py:17
  36.4 0.8 constant_dynamic-update-slice_fusion
  37.1 0.7 copy_dynamic-update-slice_fusion
  37.9 1.9 %collective-permute-start = (bf16[16,11,128]{2,1,0:T(8,128)(2,1)S(1)}, bf16[16,11,128]{2,1,0:T(8,128)(2,1)S(1)}, u32[]{:S(2)}, u32[]{:S(2)}) collective-permute-start(bf16[16,11,128]{2,1,0:T(8,128)(2,1)S(1)} %copy_dynamic-update-slice_fusion), channel_id=1, source_target_pairs={{0,1},{1,2},{2,3},{3,4},{4,5},{5,6},{6,7},{7,8},{8,9},{9,10},{10,1... | collective-permute-start | bytes 135176 | tf_op jit(solution)/shard_map/ppermute | solution.py:16
  39.8 7.9 %collective-permute-start.1 = (bf16[16,11,128]{2,1,0:T(8,128)(2,1)S(1)}, bf16[16,11,128]{2,1,0:T(8,128)(2,1)S(1)}, u32[]{:S(2)}, u32[]{:S(2)}) collective-permute-start(bf16[16,11,128]{2,1,0:T(8,128)(2,1)S(1)} %copy_dynamic-update-slice_fusion), channel_id=1, source_target_pairs={{1,0},{2,1},{3,2},{4,3},{5,4},{6,5},{7,6},{8,7},{9,8},{10,9},{11,1... | collective-permute-start | bytes 135176 | tf_op jit(solution)/shard_map/ppermute | solution.py:17
  47.7 0.7 compare_select_fusion.1
  48.4 0.1 reshape.134
  48.5 0.1 reshape.126
  48.6 0.7 dynamic_slice.18
  49.3 0.1 compare_convert_fusion
  49.4 0.8 gather_fusion.2
  50.2 0.2 slice_multiply_fusion.1
  50.5 0.7 subtract_bitcast_fusion
  51.2 0.6 pad_clamp_fusion.1
  51.8 0.7 copy.88
  52.4 0.7 copy.89
  53.2 126.5 %while.10 = (s32[]{:T(128)}, f32[2,8,8,128]{3,2,1,0:T(8,128)S(1)}, s32[2,8,27]{2,1,0:T(8,128)S(1)}, bf16[48,8,128]{2,1,0:T(8,128)(2,1)S(1)}, bf16[2,8,3,128]{3,1...) while((s32[]{:T(128)}, f32[2,8,8,128]{3,2,1,0:T(8,128)S(1)}, s32[2,8,27]{2,1,0:T(8,128)S(1)}, ...), condition=%wide.region_1.2_spmd, body=%wide.region_0.1_spmd.sunk | while | flops 102717064 | bytes 18069496 | solution.py:83
  53.2 0.1 reshape.159
  53.3 0.9 gather_fusion.1
  54.3 0.7 bitcast_convert_fusion.3
  55.0 55.6 %multiply_convert_fusion.10 = bf16[8,27,128,128]{3,2,1,0:T(8,128)(2,1)} fusion(f32[8,27,128]{2,1,0:T(8,128)S(1)} %get-tuple-element.149, f32[8,128]{1,0:T(8,128)S(1)} %get-tuple-element.150, f32[8,27,128]{2,1,0:T(8,128)S(1)} %get-tuple-element.151, f32[8,128]{1,0:T(8,128)S(1)} %get-tuple-element.152, ...), kind=kLoop, calls=%fused_computation.4.clone.clone.clone.clone.clone.clone.1.clone.1 | loop fusion | flops 46006272 | bytes 7421952 | tf_op jit(solution)/shard_map/while/body/eval_jaxpr/bemn,bewn->bwm/dot_general | solution.py:81
  110.6 0.8 gather_fusion
  111.4 5.0 %fusion.33 = f32[2,8,8,128]{3,2,1,0:T(8,128)S(1)} fusion(f32[2,8,8,128]{3,2,1,0:T(8,128)S(1)} %get-tuple-element.163, s32[]{:T(128)} %get-tuple-element.162, bf16[8,27,8,128]{3,2,1,0:T(8,128)(2,1)S(1)} %bitcast.113, bf16[8,27,128,128]{3,2,1,0:T(8,128)(2,1)} %multiply_convert_fusion.10), kind=kOutput, calls=%fused_computation.7.clone.2 | convolution fusion | flops 56623104 | bytes 7553028 | tf_op jit(solution)/shard_map/while/body/eval_jaxpr/bemn,bewn->bwm/dot_general | solution.py:81
  116.4 0.1 reshape.159
  116.5 0.9 gather_fusion.1
  117.6 0.7 bitcast_convert_fusion.3
  118.3 55.6 %multiply_convert_fusion.10 = bf16[8,27,128,128]{3,2,1,0:T(8,128)(2,1)} fusion(f32[8,27,128]{2,1,0:T(8,128)S(1)} %get-tuple-element.149, f32[8,128]{1,0:T(8,128)S(1)} %get-tuple-element.150, f32[8,27,128]{2,1,0:T(8,128)S(1)} %get-tuple-element.151, f32[8,128]{1,0:T(8,128)S(1)} %get-tuple-element.152, ...), kind=kLoop, calls=%fused_computation.4.clone.clone.clone.clone.clone.clone.1.clone.1 | loop fusion | flops 46006272 | bytes 7421952 | tf_op jit(solution)/shard_map/while/body/eval_jaxpr/bemn,bewn->bwm/dot_general | solution.py:81
  173.9 0.8 gather_fusion
  174.7 5.0 %fusion.33 = f32[2,8,8,128]{3,2,1,0:T(8,128)S(1)} fusion(f32[2,8,8,128]{3,2,1,0:T(8,128)S(1)} %get-tuple-element.163, s32[]{:T(128)} %get-tuple-element.162, bf16[8,27,8,128]{3,2,1,0:T(8,128)(2,1)S(1)} %bitcast.113, bf16[8,27,128,128]{3,2,1,0:T(8,128)(2,1)} %multiply_convert_fusion.10), kind=kOutput, calls=%fused_computation.7.clone.2 | convolution fusion | flops 56623104 | bytes 7553028 | tf_op jit(solution)/shard_map/while/body/eval_jaxpr/bemn,bewn->bwm/dot_general | solution.py:81
  179.7 0.6 copy-done.2
  180.3 0.8 copy-done.1
  181.1 1.4 pad_maximum_fusion
  182.5 0.0 copy-start.3
  182.5 1.8 gather_fusion.3
  184.3 1.5 bitcast_convert_fusion.1
  185.8 1.3 subtract_reduce_fusion
  187.2 0.1 add_convert_fusion
  187.3 0.2 convolution_convert_fusion.2
  187.5 0.2 convolution_convert_fusion.1
  187.8 1.7 fusion.6
  (30 shorter events, 0.3 us)
Async XLA Ops:
  0.0 49.4 %copy-start = (f32[316,2,512]{2,1,0:T(2,128)S(1)}, f32[316,2,512]{2,1,0:T(2,128)}, u32[]{:S(2)}) copy-start(f32[316,2,512]{2,1,0:T(2,128)} %param.23) | copy-start | bytes 3883012
  28.4 151.2 %collective-permute-start.2 = (bf16[32,2,8,512]{3,2,1,0:T(8,128)(2,1)S(1)}, bf16[32,2,8,512]{3,2,1,0:T(8,128)(2,1)S(1)}, u32[]{:S(2)}, u32[]{:S(2)}) collective-permute-start(bf16[32,2,8,512]{3,2,1,0:T(8,128)(2,1)S(1)} %all_gather.3), channel_id=1, source_target_pairs={{0,16},{16,32},{32,48},{48,64},{64,80},{80,96},{96,112},{112,128},... | collective-permute-start | bytes 1572872 | tf_op jit(solution)/shard_map/ppermute | solution.py:16
  31.9 149.2 %collective-permute-start.3 = (bf16[32,2,8,512]{3,2,1,0:T(8,128)(2,1)S(1)}, bf16[32,2,8,512]{3,2,1,0:T(8,128)(2,1)}, u32[]{:S(2)}, u32[]{:S(2)}) collective-permute-start(bf16[32,2,8,512]{3,2,1,0:T(8,128)(2,1)S(1)} %all_gather.3), channel_id=1, source_target_pairs={{16,0},{32,16},{48,32},{64,48},{80,64},{96,80},{112,96},{128,112},... | collective-permute-start | bytes 1572872 | tf_op jit(solution)/shard_map/ppermute | solution.py:17
  37.9 15.2 %collective-permute-start = (bf16[16,11,128]{2,1,0:T(8,128)(2,1)S(1)}, bf16[16,11,128]{2,1,0:T(8,128)(2,1)S(1)}, u32[]{:S(2)}, u32[]{:S(2)}) collective-permute-start(bf16[16,11,128]{2,1,0:T(8,128)(2,1)S(1)} %copy_dynamic-update-slice_fusion), channel_id=1, source_target_pairs={{0,1},{1,2},{2,3},{3,4},{4,5},{5,6},{6,7},{7,8},{8,9},{9,10},{10,1... | collective-permute-start | bytes 135176 | tf_op jit(solution)/shard_map/ppermute | solution.py:16
  39.8 13.3 %collective-permute-start.1 = (bf16[16,11,128]{2,1,0:T(8,128)(2,1)S(1)}, bf16[16,11,128]{2,1,0:T(8,128)(2,1)S(1)}, u32[]{:S(2)}, u32[]{:S(2)}) collective-permute-start(bf16[16,11,128]{2,1,0:T(8,128)(2,1)S(1)} %copy_dynamic-update-slice_fusion), channel_id=1, source_target_pairs={{1,0},{2,1},{3,2},{4,3},{5,4},{6,5},{7,6},{8,7},{9,8},{10,9},{11,1... | collective-permute-start | bytes 135176 | tf_op jit(solution)/shard_map/ppermute | solution.py:17
  179.7 0.6 copy-start.2
  180.3 0.8 copy-start.1
  182.5 5.3 %copy-start.3 = (f32[2,8,8,128]{3,2,1,0:T(8,128)S(1)}, f32[2,8,8,128]{3,2,1,0:T(8,128)}, u32[]{:S(2)}) copy-start(f32[2,8,8,128]{3,2,1,0:T(8,128)} %copy-done.2) | copy-start | bytes 196612
where the time goes:
time: 190 us; the launch traced here: 189 us
  other arithmetic  121 us (64%)
  blocking collectives  24.6 us (13%)
  starting transfers between devices  17.7 us (9%)
  matrix products  13.5 us (7%)
  local copies, waits for them, and re-layouts  12.3 us (6%)
    dot_general x2, other arithmetic, near_block(): jnp.einsum('bemn,bewn->bwm', tiles, src_x, preferred_element_type=jnp.flo...  111 us
    all_gather x1, blocking collectives, per_device(): group_spec = lax.all_gather(parent, 'dir', axis=0, tiled=True)  24.6 us
    ppermute x2, starting transfers between devices, extended(): after = lax.ppermute(first, axis, down)  12.3 us
    dot_general x2, matrix products, near_block(): jnp.einsum('bemn,bewn->bwm', tiles, src_x, preferred_element_type=jnp.flo...  9.99 us
    ppermute x2, starting transfers between devices, extended(): before = lax.ppermute(last, axis, up)  5.39 us
  transfers between devices with their start and end apart: 4, of which 0 were waited for; matrix products, arithmetic and copies ran while one was open for 70% of the time, Pallas kernels for 0%

commit v1 on v0

v1 whole, which is shorter than its diff:
```python
import functools
import math

import jax
import jax.numpy as jnp
from jax import lax
from jax.experimental import pallas as pl
from jax.experimental.pallas import tpu as pltpu
from jax.sharding import PartitionSpec as P

F = jnp.float32
BF = jnp.bfloat16
MESH = pl.DeviceIdType.MESH
NT_DIMS = (((1,), (1,)), ((), ()))

TURN = 4.0 / (2.0 * math.pi)
SIN_TURN = (6.283164044284151, -41.33714236874864, 81.34076881229882, -70.99343258230081)
SIN_TURN_LONG = (
    6.283185160089382,
    -41.34165503139618,
    81.60100407210419,
    -76.54978226888187,
    39.536705889889106,
)
TINY = 2e-6

SPREAD_AT = 2
TRANSLATE_AT = 5
RETURN_AT = 6


def cos_turns(turns):
    z = 0.25 - jnp.abs(turns - jnp.round(turns))
    v = z * z
    acc = jnp.full_like(v, SIN_TURN_LONG[-1])
    for c in SIN_TURN_LONG[-2::-1]:
        acc = acc * v + c
    return acc * z


def near_tile(dist_sq):
    turns = dist_sq * lax.rsqrt(jnp.maximum(dist_sq, TINY))
    z = 0.25 - jnp.abs(turns - jnp.round(turns))
    ratio = (z / (turns + 0.5 * TURN)).astype(BF)
    v = z.astype(BF)
    v = v * v
    coefs = [jnp.asarray(c / math.pi, BF) for c in SIN_TURN]
    acc = v * coefs[-1] + coefs[-2]
    for c in coefs[-3::-1]:
        acc = acc * v + c
    return acc * ratio


def inside(index, size):
    return jnp.minimum(jnp.maximum(index, 0), size - 1)


def three_parts(x):
    high = x.astype(BF).astype(F)
    rest = x - high
    mid = rest.astype(BF).astype(F)
    return high, mid, rest - mid


def kernel(
    dims,
    near_src,
    trans_src,
    trans_id,
    trans_count,
    cur,
    pos,
    rad,
    idx,
    wgt,
    phase,
    table,
    out,
    halo_x,
    halo_p,
    tab,
    imat,
    stage,
    window,
    loc,
    back,
    rows32,
    own32,
    src_tab,
    x_tab,
    own_tab,
    near,
    tab_sem,
    hs_sem,
    hr_sem,
    gs_sem,
    gr_sem,
    ss_sem,
    sr_sem,
    bs_sem,
    br_sem,
):
    n_box, n_dir, boxes, entries, trans_entries, ops = dims
    box = lax.axis_index("box")
    d = lax.axis_index("dir")
    me = box * n_dir + d
    n_dev = n_box * n_dir
    quarter = lax.rem(d, 4)
    fourth = d // 4
    nxt = lax.rem(me + 1, n_dev)
    prv = lax.rem(me + n_dev - 1, n_dev)
    nxt_id = (nxt // n_dir, lax.rem(nxt, n_dir))
    prv_id = (prv // n_dir, lax.rem(prv, n_dir))
    up_id = (lax.rem(box + 1, n_box), d)
    down_id = (lax.rem(box + n_box - 1, n_box), d)

    def peer(k):
        return lax.rem(d + k, n_dir)

    barrier = pltpu.get_barrier_semaphore()
    for to in (nxt_id, prv_id, up_id, down_id):
        pl.semaphore_signal(barrier, inc=1, device_id=to, device_id_type=MESH)
    for k in range(1, n_dir):
        pl.semaphore_signal(barrier, inc=1, device_id=(box, peer(k)), device_id_type=MESH)

    lanes = pl.ds(pl.multiple_of(quarter * 128, 128), 128)
    tab_copy = pltpu.make_async_copy(table.at[:, :, lanes], tab.at[pl.ds(0, ops)], tab_sem)
    tab_copy.start()

    row = lax.broadcasted_iota(jnp.int32, (128, 512), 0)
    acc = jnp.zeros((128, 512), F)
    for s in range(4):
        acc = acc + jnp.where(idx[s : s + 1, :] == row, wgt[s : s + 1, :], 0.0)
    imat[...] = acc.astype(BF)
    leaf = jnp.dot(cur[...], rad[...], preferred_element_type=F).astype(BF)

    pl.semaphore_wait(barrier, n_dir + 3)

    def halo(side, to):
        return (
            pltpu.make_async_remote_copy(
                src_ref=cur,
                dst_ref=halo_x.at[side],
                send_sem=hs_sem.at[side],
                recv_sem=hr_sem.at[side],
                device_id=to,
                device_id_type=MESH,
            ),
            pltpu.make_async_remote_copy(
                src_ref=pos,
                dst_ref=halo_p.at[side],
                send_sem=hs_sem.at[2 + side],
                recv_sem=hr_sem.at[2 + side],
                device_id=to,
                device_id_type=MESH,
            ),
        )

    halos = halo(0, nxt_id) + halo(1, prv_id)
    for c in halos:
        c.start()

    up_re = jnp.dot(leaf[:, :128], imat[...], preferred_element_type=F)
    up_im = jnp.dot(leaf[:, 128:], imat[...], preferred_element_type=F)
    turns = phase[...] * (1.0 / (2.0 * math.pi))
    cosp = cos_turns(turns)
    sinp = cos_turns(turns - 0.25)
    for q in range(2):
        re = jnp.zeros((8, 512), F)
        im = jnp.zeros((8, 512), F)
        for c in range(8):
            at = 64 * q + 8 * c
            cc, sc = cosp[c : c + 1, :], sinp[c : c + 1, :]
            ur, ui = up_re[at : at + 8], up_im[at : at + 8]
            re = re + (cc * ur - sc * ui)
            im = im + (sc * ur + cc * ui)
        both = jnp.concatenate([re, im], axis=0).astype(BF)
        for a in range(4):
            stage[a, q] = both[:, 128 * a : 128 * a + 128]

    def tables(block, positions):
        p = [positions[k].astype(F) for k in range(3)]
        norm = (p[0] * p[0] + p[1] * p[1] + p[2] * p[2]) * (TURN * TURN)
        parts = three_parts(norm)
        one = jnp.ones_like(norm)
        for k in range(3):
            for j in range(3):
                rows32[3 * j + k, block] = p[k]
            rows32[9 + k, block] = one
            rows32[12 + k, block] = parts[k]
        rows32[15, block] = jnp.zeros_like(norm)
        if block == 1:
            for k in range(3):
                scaled = three_parts(p[k] * (-2.0 * TURN * TURN))
                for j in range(3):
                    own32[3 * j + k] = scaled[j]
                own32[9 + k] = parts[k]
                own32[12 + k] = one
            own32[15] = jnp.zeros_like(norm)

    def currents_of(block, values):
        for i in range(boxes // 2):
            pair = values[16 * i : 16 * i + 16].astype(F)
            for h in range(2):
                one_box = pair[8 * h : 8 * h + 8]
                x_tab[block * boxes + 2 * i + h] = jnp.concatenate(
                    [one_box, jnp.zeros_like(one_box)], axis=0
                ).astype(BF)

    tables(1, pos)
    currents_of(1, cur)

    def own_step(i, carry):
        own_tab[i] = own32[:, i, :].T.astype(BF)
        return carry

    lax.fori_loop(0, boxes, own_step, 0, unroll=4)

    def group(k):
        to = peer(k)
        return pltpu.make_async_remote_copy(
            src_ref=stage.at[lax.rem(to, 4)],
            dst_ref=window.at[pl.ds(2 * n_dir + 2 * d, 2)],
            send_sem=gs_sem.at[k],
            recv_sem=gr_sem.at[k],
            device_id=(box, to),
            device_id_type=MESH,
        )

    for k in range(1, n_dir):
        group(k).start()
    window[pl.ds(2 * n_dir + 2 * d, 2)] = stage[quarter]

    for c in halos:
        c.wait()
    for side in range(2):
        tables(2 * side, halo_p.at[side])
        currents_of(2 * side, halo_x.at[side])

    for block in range(3):

        def src_step(i, carry):
            src_tab[block * boxes + i] = rows32[:, block, i, :].astype(BF)
            return carry

        lax.fori_loop(0, boxes, src_step, 0, unroll=8)

    def spread(side, to):
        return pltpu.make_async_remote_copy(
            src_ref=window.at[pl.ds(2 * n_dir, 2 * n_dir)],
            dst_ref=window.at[pl.ds(4 * n_dir * side, 2 * n_dir)],
            send_sem=ss_sem.at[side],
            recv_sem=sr_sem.at[side],
            device_id=to,
            device_id_type=MESH,
        )

    def returned(k):
        to = 4 * fourth + lax.rem(quarter + k, 4)
        return pltpu.make_async_remote_copy(
            src_ref=loc.at[lax.rem(quarter + k, 4)],
            dst_ref=back.at[quarter],
            send_sem=bs_sem.at[k],
            recv_sem=br_sem.at[k],
            device_id=(box, to),
            device_id_type=MESH,
        )

    base = (me - 1) * boxes
    pairs = entries // 2

    def boxes_step(step, carry):
        @pl.when(step == SPREAD_AT)
        def _():
            for k in range(1, n_dir):
                group(k).wait()
            spread(0, up_id).start()
            spread(1, down_id).start()

        @pl.when(step == TRANSLATE_AT)
        def _():
            spread(0, up_id).wait()
            spread(1, down_id).wait()
            tab_copy.wait()
            tab[ops] = jnp.zeros((2, 128), F)
            group_base = (box - 1) * (2 * n_dir)

            def target(r, inner):
                line = 8 * fourth + r
                count = trans_count[line]
                re = jnp.zeros((8, 128), F)
                im = jnp.zeros((8, 128), F)
                for e in range(trans_entries):
                    at = inside(trans_src[line, e] - group_base, 6 * n_dir)
                    op = jnp.where(e < count, inside(trans_id[line, e], ops), ops)
                    src = window[at].astype(F)
                    co = tab[op]
                    cr, ci = co[0:1, :], co[1:2, :]
                    re = re + (cr * src[:8] - ci * src[8:])
                    im = im + (cr * src[8:] + ci * src[:8])
                loc[r // 2, lax.rem(r, 2)] = jnp.concatenate([re, im], axis=0).astype(BF)
                return inner

            lax.fori_loop(0, 8, target, 0)

        @pl.when(step == RETURN_AT)
        def _():
            for k in range(1, 4):
                returned(k).start()
            back[quarter] = loc[quarter]

        for h in range(2):
            i = 2 * step + h
            lhs = own_tab[i]
            acc = None
            for j in range(pairs + 1):
                if j < pairs:
                    s0 = inside(near_src[i, 2 * j] - base, 3 * boxes)
                    s1 = inside(near_src[i, 2 * j + 1] - base, 3 * boxes)
                    rhs = jnp.concatenate([src_tab[s0], src_tab[s1]], axis=1)
                    x = jnp.concatenate([x_tab[s0], x_tab[s1]], axis=1)
                else:
                    s0 = inside(near_src[i, 2 * pairs] - base, 3 * boxes)
                    rhs, x = src_tab[s0], x_tab[s0]
                tile = near_tile(jnp.dot(lhs, rhs, preferred_element_type=F))
                part = lax.dot_general(tile, x, NT_DIMS, preferred_element_type=F)
                acc = part if acc is None else acc + part
            near[i] = acc.T[:8]
        return carry

    lax.fori_loop(0, boxes // 2, boxes_step, 0)

    for k in range(1, 4):
        returned(k).wait()
    down_re, down_im = [], []
    for q in range(2):
        got = jnp.concatenate([back[a, q].astype(F) for a in range(4)], axis=1)
        lr, li = got[:8], got[8:]
        for c in range(8):
            cc, sc = cosp[c : c + 1, :], sinp[c : c + 1, :]
            down_re.append(cc * lr + sc * li)
            down_im.append(cc * li - sc * lr)
    in_re = lax.dot_general(
        jnp.concatenate(down_re, axis=0).astype(BF), imat[...], NT_DIMS, preferred_element_type=F
    )
    in_im = lax.dot_general(
        jnp.concatenate(down_im, axis=0).astype(BF), imat[...], NT_DIMS, preferred_element_type=F
    )
    incoming = jnp.concatenate([in_re, in_im], axis=1).astype(BF)
    far = lax.dot_general(incoming, rad[...], NT_DIMS, preferred_element_type=F)
    scale = 2.0 / math.sqrt(entries * 128)
    out[...] = near[...].reshape(boxes * 8, 128) * scale + far


def per_device(
    currents,
    positions,
    radiation,
    interp_index,
    interp_weight,
    child_phase,
    near_src,
    trans_src,
    trans_id,
    trans_count,
    trans_table,
):
    boxes, waves, width = currents.shape
    n_box, n_dir = lax.axis_size("box"), lax.axis_size("dir")
    ops = trans_table.shape[0]
    dims = (n_box, n_dir, boxes, near_src.shape[1], trans_src.shape[1], ops)
    smem = pl.BlockSpec(memory_space=pltpu.SMEM)
    vmem = pl.BlockSpec(memory_space=pltpu.VMEM)
    dma = pltpu.SemaphoreType.DMA
    field = pl.pallas_call(
        functools.partial(kernel, dims),
        out_shape=jax.ShapeDtypeStruct((boxes * waves, width), F),
        in_specs=[smem] * 4 + [vmem] * 6 + [pl.BlockSpec(memory_space=pl.ANY)],
        out_specs=vmem,
        scratch_shapes=[
            pltpu.VMEM((2, boxes * waves, width), BF),
            pltpu.VMEM((2, 3, boxes, width), BF),
            pltpu.VMEM((ops + 1, 2, 128), F),
            pltpu.VMEM((128, 512), BF),
            pltpu.VMEM((4, 2, 16, 128), BF),
            pltpu.VMEM((6 * n_dir, 16, 128), BF),
            pltpu.VMEM((4, 2, 16, 128), BF),
            pltpu.VMEM((4, 2, 16, 128), BF),
            pltpu.VMEM((16, 3, boxes, 128), F),
            pltpu.VMEM((16, boxes, 128), F),
            pltpu.VMEM((3 * boxes, 16, 128), BF),
            pltpu.VMEM((3 * boxes, 16, 128), BF),
            pltpu.VMEM((boxes, 128, 16), BF),
            pltpu.VMEM((boxes, 8, 128), F),
            dma,
            dma((4,)),
            dma((4,)),
            dma((16,)),
            dma((16,)),
            dma((2,)),
            dma((2,)),
            dma((4,)),
            dma((4,)),
        ],
        compiler_params=pltpu.CompilerParams(
            collective_id=0, has_side_effects=True, vmem_limit_bytes=48 * 1024 * 1024
        ),
        name="mlfma",
    )(
        near_src,
        trans_src,
        trans_id,
        trans_count,
        currents.reshape(boxes * waves, width),
        positions.transpose(1, 0, 2),
        radiation,
        interp_index.T,
        interp_weight.T,
        child_phase,
        trans_table,
    )
    return field.reshape(boxes, waves, width)


def solution(mesh):
    placed = (
        P(("box", "dir"), None, None),
        P(("box", "dir"), None, None),
        P(),
        P(),
        P(),
        P(),
        P(("box", "dir"), None),
        P("box", None),
        P("box", None),
        P("box"),
        P(),
    )
    return jax.shard_map(
        per_device,
        mesh=mesh,
        in_specs=placed,
        out_specs=P(("box", "dir"), None, None),
        check_vma=False,
    )
```

time: 190 us -> 49 us (0.26)
  the two profiles are of different devices: /device:TPU:4 before, /device:TPU:1 now
where the time goes in v1:
time: 49 us; the launch traced here: 48.4 us
  Pallas kernels  39.2 us (80%)
  local copies, waits for them, and re-layouts  9.14 us (19%)
    pallas_call x1, Pallas kernels, per_device(): pl.pallas_call(functools.partial(kernel, dims), out_shape=jax.ShapeDtypeS...  39.2 us
    unnamed x23, local copies, waits for them, and re-layouts  9.14 us

profile of v1, /device:TPU:1, one launch (start us, length us, event | category | flops | bytes accessed | tf_op | source)
XLA Modules:
  0.0 48.4 jit_solution(14245136735025720766)
XLA Ops:
  0.0 0.0 copy-start
  0.0 1.3 %copy-done = f32[316,2,512]{2,1,0:T(2,128)S(1)} copy-done((f32[316,2,512]{2,1,0:T(2,128)S(1)}, f32[316,2,512]{2,1,0:T(2,128)}, u32[]{:S(2)}) %copy-start) | copy-done | bytes 1294360
  1.3 0.0 copy-start.1
  1.3 0.8 %copy-done.1 = bf16[128,256]{1,0:T(8,128)(2,1)S(1)} copy-done((bf16[128,256]{1,0:T(8,128)(2,1)S(1)}, bf16[128,256]{1,0:T(8,128)(2,1)}, u32[]{:S(2)}) %copy-start.1) | copy-done | bytes 65560
  2.2 0.0 copy-start.2
  2.2 0.8 %copy-done.2 = bf16[16,8,128]{2,1,0:T(8,128)(2,1)S(1)} copy-done((bf16[16,8,128]{2,1,0:T(8,128)(2,1)S(1)}, bf16[16,8,128]{2,1,0:T(8,128)(2,1)}, u32[]{:S(2)}) %copy-start.2) | copy-done | bytes 32792
  2.9 0.0 copy-start.3
  2.9 0.7 %copy-done.3 = s32[32,32]{1,0:T(8,128)S(1)} copy-done((s32[32,32]{1,0:T(8,128)S(1)}, s32[32,32]{1,0:T(8,128)}, u32[]{:S(2)}) %copy-start.3) | copy-done | bytes 4120
  3.6 0.0 copy-start.4
  3.6 0.7 %copy-done.4 = s32[32,32]{1,0:T(8,128)S(1)} copy-done((s32[32,32]{1,0:T(8,128)S(1)}, s32[32,32]{1,0:T(8,128)}, u32[]{:S(2)}) %copy-start.4) | copy-done | bytes 4120
  4.3 0.0 copy-start.5
  4.3 0.7 %copy-done.5 = f32[8,512]{1,0:T(8,128)S(1)} copy-done((f32[8,512]{1,0:T(8,128)S(1)}, f32[8,512]{1,0:T(8,128)}, u32[]{:S(2)}) %copy-start.5) | copy-done | bytes 16408
  5.1 0.0 copy-start.6
  5.1 0.7 %copy-done.6 = bf16[16,3,128]{2,0,1:T(8,128)(2,1)S(1)} copy-done((bf16[16,3,128]{2,0,1:T(8,128)(2,1)S(1)}, bf16[16,3,128]{2,0,1:T(8,128)(2,1)}, u32[]{:S(2)}) %copy-start.6) | copy-done | bytes 12312
  5.8 0.0 copy-start.7
  5.8 0.7 %copy-done.7 = s32[16,27]{1,0:T(8,128)S(1)} copy-done((s32[16,27]{1,0:T(8,128)S(1)}, s32[16,27]{1,0:T(8,128)}, u32[]{:S(2)}) %copy-start.7) | copy-done | bytes 1752
  6.5 0.0 copy-start.8
  6.5 0.7 %copy-done.8 = s32[512,4]{0,1:T(4,128)S(1)} copy-done((s32[512,4]{0,1:T(4,128)S(1)}, s32[512,4]{0,1:T(4,128)}, u32[]{:S(2)}) %copy-start.8) | copy-done | bytes 8216
  7.2 0.0 copy-start.9
  7.2 0.7 %copy-done.9 = f32[512,4]{0,1:T(4,128)S(1)} copy-done((f32[512,4]{0,1:T(4,128)S(1)}, f32[512,4]{0,1:T(4,128)}, u32[]{:S(2)}) %copy-start.9) | copy-done | bytes 8216
  7.9 0.0 copy-start.10
  7.9 0.7 %copy-done.10 = s32[32]{0:T(128)S(1)} copy-done((s32[32]{0:T(128)S(1)}, s32[32]{0:T(128)}, u32[]{:S(2)}) %copy-start.10) | copy-done | bytes 152
  8.5 39.2 %mlfma.1 = f32[128,128]{1,0:T(8,128)S(1)} custom-call(s32[16,27]{1,0:T(8,128)S(1)} %copy-done.7, s32[32,32]{1,0:T(8,128)S(1)} %copy-done.3, s32[32,32]{1,0:T(8,128)S(1)} %copy-done.4, s32[32]{0:T(128)S(1)} %copy-done.10, bf16[128,128]{1,0:T(8,128)(2,1)S(1)} %bitcast.6, bf16[3,16,128]{2,1,0:T(8,128)(2,1)S(1)} %bitcast.7, bf16[128,256]{1,0:T(8,128)(2,1)S(1)} %copy-done.1, ...), custom_call_target="tpu_custom_call" | custom-call | tf_op jit(solution)/shard_map/mlfma/pallas_call | solution.py:375
  47.7 0.6 %copy.13 = f32[16,8,128]{2,1,0:T(8,128)} copy(f32[16,8,128]{2,1,0:T(8,128)S(1)} %bitcast.5) | data formatting | bytes 131072
Async XLA Ops:
  0.0 1.3 %copy-start = (f32[316,2,512]{2,1,0:T(2,128)S(1)}, f32[316,2,512]{2,1,0:T(2,128)}, u32[]{:S(2)}) copy-start(f32[316,2,512]{2,1,0:T(2,128)} %table.1) | copy-start | bytes 3883012
  1.3 0.8 %copy-start.1 = (bf16[128,256]{1,0:T(8,128)(2,1)S(1)}, bf16[128,256]{1,0:T(8,128)(2,1)}, u32[]{:S(2)}) copy-start(bf16[128,256]{1,0:T(8,128)(2,1)} %rad.1) | copy-start | bytes 196612
  2.2 0.8 %copy-start.2 = (bf16[16,8,128]{2,1,0:T(8,128)(2,1)S(1)}, bf16[16,8,128]{2,1,0:T(8,128)(2,1)}, u32[]{:S(2)}) copy-start(bf16[16,8,128]{2,1,0:T(8,128)(2,1)} %param.11) | copy-start | bytes 98308
  2.9 0.7 %copy-start.3 = (s32[32,32]{1,0:T(8,128)S(1)}, s32[32,32]{1,0:T(8,128)}, u32[]{:S(2)}) copy-start(s32[32,32]{1,0:T(8,128)} %trans_src.1) | copy-start | bytes 12292
  3.6 0.7 %copy-start.4 = (s32[32,32]{1,0:T(8,128)S(1)}, s32[32,32]{1,0:T(8,128)}, u32[]{:S(2)}) copy-start(s32[32,32]{1,0:T(8,128)} %trans_id.1) | copy-start | bytes 12292
  4.3 0.7 %copy-start.5 = (f32[8,512]{1,0:T(8,128)S(1)}, f32[8,512]{1,0:T(8,128)}, u32[]{:S(2)}) copy-start(f32[8,512]{1,0:T(8,128)} %phase.1) | copy-start | bytes 49156
  5.1 0.7 %copy-start.6 = (bf16[16,3,128]{2,0,1:T(8,128)(2,1)S(1)}, bf16[16,3,128]{2,0,1:T(8,128)(2,1)}, u32[]{:S(2)}) copy-start(bf16[16,3,128]{2,0,1:T(8,128)(2,1)} %param.12) | copy-start | bytes 36868
  5.8 0.7 %copy-start.7 = (s32[16,27]{1,0:T(8,128)S(1)}, s32[16,27]{1,0:T(8,128)}, u32[]{:S(2)}) copy-start(s32[16,27]{1,0:T(8,128)} %near_src.1) | copy-start | bytes 5188
  6.5 0.7 %copy-start.8 = (s32[512,4]{0,1:T(4,128)S(1)}, s32[512,4]{0,1:T(4,128)}, u32[]{:S(2)}) copy-start(s32[512,4]{0,1:T(4,128)} %param.14) | copy-start | bytes 24580
  7.2 0.7 %copy-start.9 = (f32[512,4]{0,1:T(4,128)S(1)}, f32[512,4]{0,1:T(4,128)}, u32[]{:S(2)}) copy-start(f32[512,4]{0,1:T(4,128)} %param.15) | copy-start | bytes 24580
  7.9 0.7 %copy-start.10 = (s32[32]{0:T(128)S(1)}, s32[32]{0:T(128)}, u32[]{:S(2)}) copy-start(s32[32]{0:T(128)} %trans_count.1) | copy-start | bytes 388

commit v2 on v1

v2 whole, which is shorter than its diff:
```python
import functools
import math

import jax
import jax.numpy as jnp
from jax import lax
from jax.experimental import pallas as pl
from jax.experimental.pallas import tpu as pltpu
from jax.sharding import PartitionSpec as P

F = jnp.float32
BF = jnp.bfloat16
MESH = pl.DeviceIdType.MESH
NT_DIMS = (((1,), (1,)), ((), ()))

TURN = 4.0 / (2.0 * math.pi)
SIN_TURN = (6.283164044284151, -41.33714236874864, 81.34076881229882, -70.99343258230081)
SIN_TURN_LONG = (
    6.283185160089382,
    -41.34165503139618,
    81.60100407210419,
    -76.54978226888187,
    39.536705889889106,
)
TINY = 2e-6

STRIDE = 4


def cos_turns(turns):
    z = 0.25 - jnp.abs(turns - jnp.round(turns))
    v = z * z
    acc = jnp.full_like(v, SIN_TURN_LONG[-1])
    for c in SIN_TURN_LONG[-2::-1]:
        acc = acc * v + c
    return acc * z


def near_tile(dist_sq):
    turns = dist_sq * lax.rsqrt(jnp.maximum(dist_sq, TINY))
    z = 0.25 - jnp.abs(turns - jnp.round(turns))
    ratio = (z / (turns + 0.5 * TURN)).astype(BF)
    v = z.astype(BF)
    v = v * v
    coefs = [jnp.asarray(c / math.pi, BF) for c in SIN_TURN]
    acc = v * coefs[-1] + coefs[-2]
    for c in coefs[-3::-1]:
        acc = acc * v + c
    return acc * ratio


def inside(index, size):
    return jnp.minimum(jnp.maximum(index, 0), size - 1)


def three_parts(x):
    high = x.astype(BF).astype(F)
    rest = x - high
    mid = rest.astype(BF).astype(F)
    return high, mid, rest - mid


def prepare_kernel(
    dims,
    cur_in,
    pos_in,
    rad_in,
    idx_in,
    wgt_in,
    phase_in,
    near_in,
    src_in,
    id_in,
    near_list,
    src_list,
    id_list,
    src_tab,
    x_tab,
    own_tab,
    stage,
    imat,
    cosp,
    sinp,
    cur,
    pos,
    rad,
    idx,
    wgt,
    phase,
    near_src,
    trans_src,
    trans_id,
    halo_x,
    halo_p,
    rows32,
    own32,
    in_sem,
    hs_sem,
    hr_sem,
):
    n_box, n_dir, boxes, ops = dims
    me = lax.axis_index("box") * n_dir + lax.axis_index("dir")
    n_dev = n_box * n_dir
    nxt = lax.rem(me + 1, n_dev)
    prv = lax.rem(me + n_dev - 1, n_dev)
    nxt_id = (nxt // n_dir, lax.rem(nxt, n_dir))
    prv_id = (prv // n_dir, lax.rem(prv, n_dir))

    has_nxt, has_prv = me < n_dev - 1, me > 0
    barrier = pltpu.get_barrier_semaphore()
    for has, to in ((has_nxt, nxt_id), (has_prv, prv_id)):

        @pl.when(has)
        def _():
            pl.semaphore_signal(barrier, inc=1, device_id=to, device_id_type=MESH)

    moves = [
        pltpu.make_async_copy(a, b, in_sem.at[k])
        for k, (a, b) in enumerate(
            [
                (cur_in, cur),
                (pos_in, pos),
                (idx_in, idx),
                (wgt_in, wgt),
                (rad_in, rad),
                (phase_in, phase),
                (near_in, near_src),
                (src_in, trans_src),
                (id_in, trans_id),
            ]
        )
    ]
    for m in moves:
        m.start()

    def halo(side, to):
        return (
            pltpu.make_async_remote_copy(
                src_ref=cur_in,
                dst_ref=halo_x.at[side],
                send_sem=hs_sem.at[side],
                recv_sem=hr_sem.at[side],
                device_id=to,
                device_id_type=MESH,
            ),
            pltpu.make_async_remote_copy(
                src_ref=pos_in,
                dst_ref=halo_p.at[side],
                send_sem=hs_sem.at[2 + side],
                recv_sem=hr_sem.at[2 + side],
                device_id=to,
                device_id_type=MESH,
            ),
        )

    pl.semaphore_wait(barrier, has_nxt.astype(jnp.int32) + has_prv.astype(jnp.int32))

    for side, has, to in ((0, has_nxt, nxt_id), (1, has_prv, prv_id)):

        @pl.when(has)
        def _():
            for c in halo(side, to):
                c.start()

    for m in moves:
        m.wait()
    near_list[...] = inside(near_src[...] - (me - 1) * boxes, 3 * boxes)
    group_base = (lax.axis_index("box") - 1) * (2 * n_dir)
    src_list[...] = inside(trans_src[...] - group_base, 6 * n_dir)
    id_list[...] = inside(trans_id[...], ops)
    row = lax.broadcasted_iota(jnp.int32, (128, 512), 0)
    acc = jnp.zeros((128, 512), F)
    for s in range(4):
        acc = acc + jnp.where(idx[s : s + 1, :] == row, wgt[s : s + 1, :], 0.0)
    imat[...] = acc.astype(BF)

    leaf = jnp.dot(cur[...], rad[...], preferred_element_type=F).astype(BF)
    up_re = jnp.dot(leaf[:, :128], imat[...], preferred_element_type=F)
    up_im = jnp.dot(leaf[:, 128:], imat[...], preferred_element_type=F)
    turns = phase[...] * (1.0 / (2.0 * math.pi))
    cosv = cos_turns(turns)
    sinv = cos_turns(turns - 0.25)
    cosp[...] = cosv
    sinp[...] = sinv
    for q in range(2):
        re = jnp.zeros((8, 512), F)
        im = jnp.zeros((8, 512), F)
        for c in range(8):
            at = 64 * q + 8 * c
            cc, sc = cosv[c : c + 1, :], sinv[c : c + 1, :]
            ur, ui = up_re[at : at + 8], up_im[at : at + 8]
            re = re + (cc * ur - sc * ui)
            im = im + (sc * ur + cc * ui)
        both = jnp.concatenate([re, im], axis=0).astype(BF)
        for a in range(4):
            stage[a, q] = both[:, 128 * a : 128 * a + 128]

    width = 3 * boxes

    def tables(block, positions):
        def put(k, value):
            rows32[k * width + block * boxes : k * width + (block + 1) * boxes] = value

        def put_own(k, value):
            own32[k * boxes : (k + 1) * boxes] = value

        p = [positions[k].astype(F) for k in range(3)]
        norm = (p[0] * p[0] + p[1] * p[1] + p[2] * p[2]) * (TURN * TURN)
        parts = three_parts(norm)
        one = jnp.ones_like(norm)
        for k in range(3):
            for j in range(3):
                put(3 * j + k, p[k])
            put(9 + k, one)
            put(12 + k, parts[k])
        put(15, jnp.zeros_like(norm))
        if block == 1:
            for k in range(3):
                scaled = three_parts(p[k] * (-2.0 * TURN * TURN))
                for j in range(3):
                    put_own(3 * j + k, scaled[j])
                put_own(9 + k, parts[k])
                put_own(12 + k, one)
            put_own(15, jnp.zeros_like(norm))
        for i in range(boxes):
            src_tab[block * boxes + i] = rows32[
                pl.ds(block * boxes + i, 16, stride=width), :
            ].astype(BF)

    def currents_of(block, values):
        for i in range(boxes // 2):
            pair = values[16 * i : 16 * i + 16].astype(F)
            for h in range(2):
                one_box = pair[8 * h : 8 * h + 8]
                x_tab[block * boxes + 2 * i + h] = jnp.concatenate(
                    [one_box, jnp.zeros_like(one_box)], axis=0
                ).astype(BF)

    tables(1, pos)
    currents_of(1, cur)
    for i in range(boxes):
        own_tab[i] = own32[pl.ds(i, 16, stride=boxes), :].T.astype(BF)

    for side, to_has, to, from_has in (
        (0, has_nxt, nxt_id, has_prv),
        (1, has_prv, prv_id, has_nxt),
    ):

        @pl.when(to_has)
        def _():
            for c in halo(side, to):
                c.wait_send()

        @pl.when(from_has)
        def _():
            for c in halo(side, to):
                c.wait_recv()

        @pl.when(jnp.logical_not(from_has))
        def _():
            halo_x[side] = jnp.zeros_like(halo_x[side])
            halo_p[side] = jnp.zeros_like(halo_p[side])

    for side in range(2):
        tables(2 * side, halo_p.at[side])
        currents_of(2 * side, halo_x.at[side])


def field_kernel(
    dims,
    near_list,
    src_list,
    id_list,
    src_tab,
    x_tab,
    own_tab,
    stage,
    imat,
    cosp,
    sinp,
    rad_in,
    count_in,
    table_in,
    out,
    rad,
    trans_src,
    trans_id,
    trans_count,
    tab,
    window,
    loc,
    back,
    near,
    ahead,
    in_sem,
    gs_sem,
    gr_sem,
    ss_sem,
    sr_sem,
    bs_sem,
    br_sem,
):
    n_box, n_dir, boxes, entries, trans_entries, ops = dims
    box = lax.axis_index("box")
    d = lax.axis_index("dir")
    quarter = lax.rem(d, 4)
    fourth = d // 4
    up_id = (lax.rem(box + 1, n_box), d)
    down_id = (lax.rem(box + n_box - 1, n_box), d)

    def peer(k):
        return lax.rem(d + k, n_dir)

    barrier = pltpu.get_barrier_semaphore()
    for to in (up_id, down_id):
        pl.semaphore_signal(barrier, inc=1, device_id=to, device_id_type=MESH)
    for k in range(1, n_dir):
        pl.semaphore_signal(barrier, inc=1, device_id=(box, peer(k)), device_id_type=MESH)

    lanes = pl.ds(pl.multiple_of(quarter * 128, 128), 128)
    moves = [
        pltpu.make_async_copy(a, b, in_sem.at[k])
        for k, (a, b) in enumerate(
            [
                (table_in.at[:, :, lanes], tab.at[pl.ds(0, ops)]),
                (src_list, trans_src),
                (id_list, trans_id),
                (count_in, trans_count),
                (rad_in, rad),
            ]
        )
    ]
    for m in moves:
        m.start()

    def group(k):
        to = peer(k)
        return pltpu.make_async_remote_copy(
            src_ref=stage.at[lax.rem(to, 4)],
            dst_ref=window.at[pl.ds(2 * n_dir + 2 * d, 2)],
            send_sem=gs_sem.at[k],
            recv_sem=gr_sem.at[k],
            device_id=(box, to),
            device_id_type=MESH,
        )

    def spread(side, to):
        return pltpu.make_async_remote_copy(
            src_ref=window.at[pl.ds(2 * n_dir, 2 * n_dir)],
            dst_ref=window.at[pl.ds(4 * n_dir * side, 2 * n_dir)],
            send_sem=ss_sem.at[side],
            recv_sem=sr_sem.at[side],
            device_id=to,
            device_id_type=MESH,
        )

    def returned(k):
        to = lax.rem(quarter + k, 4)
        return pltpu.make_async_remote_copy(
            src_ref=loc.at[to],
            dst_ref=back.at[quarter],
            send_sem=bs_sem.at[k],
            recv_sem=br_sem.at[k],
            device_id=(box, 4 * fourth + to),
            device_id_type=MESH,
        )

    def gather_start():
        pl.semaphore_wait(barrier, n_dir + 1)
        for k in range(1, n_dir):
            group(k).start()
        window[pl.ds(2 * n_dir + 2 * d, 2)] = stage[quarter]

    def spread_start():
        for k in range(1, n_dir):
            group(k).wait()
        spread(0, up_id).start()
        spread(1, down_id).start()

    def translate():
        spread(0, up_id).wait()
        spread(1, down_id).wait()
        for m in moves:
            m.wait()
        tab[ops] = jnp.zeros((2, 128), F)

        def target(r, inner):
            to = lax.rem(quarter + 1 + r // 2, 4)
            line = 8 * fourth + 2 * to + lax.rem(r, 2)
            count = trans_count[line]
            re = jnp.zeros((8, 128), F)
            im = jnp.zeros((8, 128), F)
            for e in range(trans_entries):
                op = jnp.where(e < count, trans_id[line, e], ops)
                src = window[trans_src[line, e]].astype(F)
                co = tab[op]
                cr, ci = co[0:1, :], co[1:2, :]
                re = re + (cr * src[:8] - ci * src[8:])
                im = im + (cr * src[8:] + ci * src[:8])
            loc[to, lax.rem(r, 2)] = jnp.concatenate([re, im], axis=0).astype(BF)
            return inner

        lax.fori_loop(0, 8, target, 0)
        for k in range(1, 4):
            returned(k).start()
        back[quarter] = loc[quarter]

    pairs = entries // 2

    def sources(i, j):
        return [near_list[i, e] for e in range(2 * j, min(2 * j + 2, entries))]

    def joined(ref, i, j):
        parts = [ref[s] for s in sources(i, j)]
        return jnp.concatenate(parts, axis=1) if len(parts) > 1 else parts[0]

    def distances(i, j):
        return jnp.dot(own_tab[i], joined(src_tab, i, j), preferred_element_type=F)

    steps = boxes // STRIDE
    first_half = jnp.logical_and(d >= 2, d < n_dir // 2)
    gather_at = jnp.where(jnp.logical_and(d >= 2, d < 3 * n_dir // 8), 2, 1)
    spread_at = jnp.where(first_half, 3, 2)
    translate_at = jnp.where(first_half, steps, 3)

    def boxes_step(step, carry):
        pl.when(step == gather_at)(gather_start)
        pl.when(step == spread_at)(spread_start)
        pl.when(step == translate_at)(translate)
        tasks = [(STRIDE * step + h, j) for h in range(STRIDE) for j in range(pairs + 1)]
        later = (jnp.minimum(STRIDE * (step + 1), boxes - 1), 0)
        dist = ahead[...]
        acc = None
        for t, (i, j) in enumerate(tasks):
            if t + 1 < len(tasks):
                dist_next = distances(*tasks[t + 1])
            else:
                ahead[...] = distances(*later)
            tile = near_tile(dist)
            part = lax.dot_general(tile, joined(x_tab, i, j), NT_DIMS, preferred_element_type=F)
            acc = part if acc is None else acc + part
            if j == pairs:
                near[i] = acc.T[:8]
                acc = None
            dist = dist_next
        return carry

    ahead[...] = distances(0, 0)
    lax.fori_loop(0, steps, boxes_step, 0)
    pl.when(translate_at == steps)(translate)

    for k in range(1, 4):
        returned(k).wait()
    down_re, down_im = [], []
    for q in range(2):
        got = jnp.concatenate([back[a, q].astype(F) for a in range(4)], axis=1)
        lr, li = got[:8], got[8:]
        for c in range(8):
            cc, sc = cosp[c : c + 1, :], sinp[c : c + 1, :]
            down_re.append(cc * lr + sc * li)
            down_im.append(cc * li - sc * lr)
    in_re = lax.dot_general(
        jnp.concatenate(down_re, axis=0).astype(BF), imat[...], NT_DIMS, preferred_element_type=F
    )
    in_im = lax.dot_general(
        jnp.concatenate(down_im, axis=0).astype(BF), imat[...], NT_DIMS, preferred_element_type=F
    )
    incoming = jnp.concatenate([in_re, in_im], axis=1).astype(BF)
    far = lax.dot_general(incoming, rad[...], NT_DIMS, preferred_element_type=F)
    scale = 2.0 / math.sqrt(entries * 128)
    out[...] = near[...].reshape(boxes * 8, 128) * scale + far


def in_hbm(x):
    return pltpu.with_memory_space_constraint(x, pltpu.HBM)


def per_device(
    currents,
    positions,
    radiation,
    interp_index,
    interp_weight,
    child_phase,
    near_src,
    trans_src,
    trans_id,
    trans_count,
    trans_table,
):
    boxes, waves, width = currents.shape
    n_box, n_dir = lax.axis_size("box"), lax.axis_size("dir")
    ops = trans_table.shape[0]
    smem = pl.BlockSpec(memory_space=pltpu.SMEM)
    vmem = pl.BlockSpec(memory_space=pltpu.VMEM)
    hbm = pl.BlockSpec(memory_space=pltpu.HBM)
    dma = pltpu.SemaphoreType.DMA
    shape = jax.ShapeDtypeStruct
    cur = currents.reshape(boxes * waves, width)
    pos = positions.transpose(1, 0, 2)
    idx = interp_index.T
    wgt = interp_weight.T
    prepared = pl.pallas_call(
        functools.partial(prepare_kernel, (n_box, n_dir, boxes, ops)),
        out_shape=[
            shape(near_src.shape, jnp.int32),
            shape(trans_src.shape, jnp.int32),
            shape(trans_id.shape, jnp.int32),
            shape((3 * boxes, 16, 128), BF),
            shape((3 * boxes, 16, 128), BF),
            shape((boxes, 128, 16), BF),
            shape((4, 2, 16, 128), BF),
            shape((128, 512), BF),
            shape((8, 512), F),
            shape((8, 512), F),
        ],
        in_specs=[hbm] * 9,
        out_specs=[vmem] * 10,
        scratch_shapes=[
            pltpu.VMEM(cur.shape, BF),
            pltpu.VMEM(pos.shape, BF),
            pltpu.VMEM(radiation.shape, BF),
            pltpu.VMEM(idx.shape, jnp.int32),
            pltpu.VMEM(wgt.shape, F),
            pltpu.VMEM(child_phase.shape, F),
            pltpu.VMEM(near_src.shape, jnp.int32),
            pltpu.VMEM(trans_src.shape, jnp.int32),
            pltpu.VMEM(trans_id.shape, jnp.int32),
            pltpu.VMEM((2,) + cur.shape, BF),
            pltpu.VMEM((2,) + pos.shape, BF),
            pltpu.VMEM((16 * 3 * boxes, 128), F),
            pltpu.VMEM((16 * boxes, 128), F),
            dma((9,)),
            dma((4,)),
            dma((4,)),
        ],
        compiler_params=pltpu.CompilerParams(
            collective_id=0, has_side_effects=True, vmem_limit_bytes=16 * 1024 * 1024
        ),
        name="prepare",
    )(
        *map(
            in_hbm,
            (cur, pos, radiation, idx, wgt, child_phase, near_src, trans_src, trans_id),
        )
    )
    dims = (n_box, n_dir, boxes, near_src.shape[1], trans_src.shape[1], ops)
    field = pl.pallas_call(
        functools.partial(field_kernel, dims),
        out_shape=shape((boxes * waves, width), F),
        in_specs=[smem] + [vmem] * 9 + [hbm] * 3,
        out_specs=vmem,
        scratch_shapes=[
            pltpu.VMEM(radiation.shape, BF),
            pltpu.SMEM(trans_src.shape, jnp.int32),
            pltpu.SMEM(trans_id.shape, jnp.int32),
            pltpu.SMEM(trans_count.shape, jnp.int32),
            pltpu.VMEM((ops + 1, 2, 128), F),
            pltpu.VMEM((6 * n_dir, 16, 128), BF),
            pltpu.VMEM((4, 2, 16, 128), BF),
            pltpu.VMEM((4, 2, 16, 128), BF),
            pltpu.VMEM((boxes, 8, 128), F),
            pltpu.VMEM((128, 256), F),
            dma((5,)),
            dma((16,)),
            dma((16,)),
            dma((2,)),
            dma((2,)),
            dma((4,)),
            dma((4,)),
        ],
        compiler_params=pltpu.CompilerParams(
            collective_id=1, has_side_effects=True, vmem_limit_bytes=32 * 1024 * 1024
        ),
        name="field",
    )(*prepared, *map(in_hbm, (radiation, trans_count, trans_table)))
    return field.reshape(boxes, waves, width)


def solution(mesh):
    placed = (
        P(("box", "dir"), None, None),
        P(("box", "dir"), None, None),
        P(),
        P(),
        P(),
        P(),
        P(("box", "dir"), None),
        P("box", None),
        P("box", None),
        P("box"),
        P(),
    )
    return jax.shard_map(
        per_device,
        mesh=mesh,
        in_specs=placed,
        out_specs=P(("box", "dir"), None, None),
        check_vma=False,
    )
```

time: 49 us -> 39.7 us (0.81); the launches traced: 48.4 us -> 39.6 us
  local copies, waits for them, and re-layouts: 9.14 us -> 0.63 us
    unnamed x23 -> x1, local copies, waits for them, and re-layouts: 9.14 us -> 0.63 us
    pallas_call x1 -> x2, Pallas kernels: 39.2 us -> 38.9 us  [the longest x1 29.8 us: per_device(): pl.pallas_call(functools.partial(field_kernel, dims), out_shape=shape((bo...]
where the time goes in v2:
time: 39.7 us; the launch traced here: 39.6 us
  Pallas kernels  38.9 us (98%)
  local copies, waits for them, and re-layouts  0.63 us (2%)
    pallas_call x1, Pallas kernels, per_device(): pl.pallas_call(functools.partial(field_kernel, dims), out_shape=shape((bo...  29.8 us
    pallas_call x1, Pallas kernels, per_device(): pl.pallas_call(functools.partial(prepare_kernel, (n_box, n_dir, boxes, op...  9.17 us

profile of v2, /device:TPU:1, one launch (start us, length us, event | category | flops | bytes accessed | tf_op | source)
XLA Modules:
  0.0 39.6 jit_solution(14735178523499528412)
XLA Ops:
  0.0 9.2 %prepare.1 = (s32[16,27]{1,0:T(8,128)S(1)}, s32[32,32]{1,0:T(8,128)S(1)}, s32[32,32]{1,0:T(8,128)S(1)}, bf16[48,16,128]{2,1,0:T(8,128)(2,1)S(1)}, bf16[48,16,128...) custom-call(bf16[128,128]{1,0:T(8,128)(2,1)} %bitcast.6, ...), custom_call_target="tpu_custom_call" | custom-call | tf_op jit(solution)/shard_map/prepare/pallas_call | solution.py:503
  9.2 29.8 %field.1 = f32[128,128]{1,0:T(8,128)S(1)} custom-call(s32[16,27]{1,0:T(8,128)S(1)} %get-tuple-element.15.near_list, s32[32,32]{1,0:T(8,128)S(1)} %get-tuple-element.16.src_list, s32[32,32]{1,0:T(8,128)S(1)} %get-tuple-element.17.id_list, bf16[48,16,128]{2,1,0:T(8,128)(2,1)S(1)} %get-tuple-element.18.src_tab, ...), custom_call_target="tpu_custom_call" | custom-call | tf_op jit(solution)/shard_map/field/pallas_call | solution.py:548
  38.9 0.6 %copy.13 = f32[16,8,128]{2,1,0:T(8,128)} copy(f32[16,8,128]{2,1,0:T(8,128)S(1)} %bitcast.5) | data formatting | bytes 131072

commit v3 on v2

--- a/solution.py
+++ b/solution.py
@@ -51,6 +51,17 @@
 
 def inside(index, size):
     return jnp.minimum(jnp.maximum(index, 0), size - 1)
+
+
+def distances(own, sources):
+    rows = jnp.concatenate(sources, axis=1) if len(sources) > 1 else sources[0]
+    return jnp.dot(own.astype(BF), rows.astype(BF), preferred_element_type=F)
+
+
+def applied(tile, currents):
+    rows = jnp.concatenate(currents, axis=1) if len(currents) > 1 else currents[0]
+    rows = jnp.concatenate([rows, jnp.zeros_like(rows)], axis=0).astype(BF)
+    return lax.dot_general(tile, rows, NT_DIMS, preferred_element_type=F)
 
 
 def three_parts(x):
@@ -77,6 +88,7 @@
     src_tab,
     x_tab,
     own_tab,
+    near_self,
     stage,
     imat,
     cosp,
@@ -223,23 +235,22 @@
                 put_own(12 + k, one)
             put_own(15, jnp.zeros_like(norm))
         for i in range(boxes):
-            src_tab[block * boxes + i] = rows32[
-                pl.ds(block * boxes + i, 16, stride=width), :
-            ].astype(BF)
+            src_tab[block * boxes + i] = rows32[pl.ds(block * boxes + i, 16, stride=width), :]
 
     def currents_of(block, values):
         for i in range(boxes // 2):
             pair = values[16 * i : 16 * i + 16].astype(F)
             for h in range(2):
-                one_box = pair[8 * h : 8 * h + 8]
-                x_tab[block * boxes + 2 * i + h] = jnp.concatenate(
-                    [one_box, jnp.zeros_like(one_box)], axis=0
-                ).astype(BF)
+                x_tab[block * boxes + 2 * i + h] = pair[8 * h : 8 * h + 8]
 
     tables(1, pos)
     currents_of(1, cur)
     for i in range(boxes):
-        own_tab[i] = own32[pl.ds(i, 16, stride=boxes), :].T.astype(BF)
+        own_tab[i] = own32[pl.ds(i, 16, stride=boxes), :].T
+
+    for i in range(boxes):
+        tile = near_tile(distances(own_tab[i], [src_tab[boxes + i]]))
+        near_self[i] = applied(tile, [x_tab[boxes + i]]).T[:8]
 
     for side, to_has, to, from_has in (
         (0, has_nxt, nxt_id, has_prv),
@@ -274,6 +285,7 @@
     src_tab,
     x_tab,
     own_tab,
+    near_self,
     stage,
     imat,
     cosp,
@@ -407,15 +419,11 @@
 
     pairs = entries // 2
 
-    def sources(i, j):
-        return [near_list[i, e] for e in range(2 * j, min(2 * j + 2, entries))]
-
-    def joined(ref, i, j):
-        parts = [ref[s] for s in sources(i, j)]
-        return jnp.concatenate(parts, axis=1) if len(parts) > 1 else parts[0]
-
-    def distances(i, j):
-        return jnp.dot(own_tab[i], joined(src_tab, i, j), preferred_element_type=F)
+    def listed(ref, i, j):
+        return [ref[near_list[i, e]] for e in range(2 * j + 1, min(2 * j + 3, entries))]
+
+    def pair_distances(i, j):
+        return distances(own_tab[i], listed(src_tab, i, j))
 
     steps = boxes // STRIDE
     first_half = jnp.logical_and(d >= 2, d < n_dir // 2)
@@ -427,25 +435,24 @@
         pl.when(step == gather_at)(gather_start)
         pl.when(step == spread_at)(spread_start)
         pl.when(step == translate_at)(translate)
-        tasks = [(STRIDE * step + h, j) for h in range(STRIDE) for j in range(pairs + 1)]
+        tasks = [(STRIDE * step + h, j) for h in range(STRIDE) for j in range(pairs)]
         later = (jnp.minimum(STRIDE * (step + 1), boxes - 1), 0)
         dist = ahead[...]
         acc = None
         for t, (i, j) in enumerate(tasks):
             if t + 1 < len(tasks):
-                dist_next = distances(*tasks[t + 1])
+                dist_next = pair_distances(*tasks[t + 1])
             else:
-                ahead[...] = distances(*later)
-            tile = near_tile(dist)
-            part = lax.dot_general(tile, joined(x_tab, i, j), NT_DIMS, preferred_element_type=F)
+                ahead[...] = pair_distances(*later)
+            part = applied(near_tile(dist), listed(x_tab, i, j))
             acc = part if acc is None else acc + part
-            if j == pairs:
+            if j == pairs - 1:
                 near[i] = acc.T[:8]
                 acc = None
             dist = dist_next
         return carry
 
-    ahead[...] = distances(0, 0)
+    ahead[...] = pair_distances(0, 0)
     lax.fori_loop(0, steps, boxes_step, 0)
     pl.when(translate_at == steps)(translate)
 
@@ -468,7 +475,7 @@
     incoming = jnp.concatenate([in_re, in_im], axis=1).astype(BF)
     far = lax.dot_general(incoming, rad[...], NT_DIMS, preferred_element_type=F)
     scale = 2.0 / math.sqrt(entries * 128)
-    out[...] = near[...].reshape(boxes * 8, 128) * scale + far
+    out[...] = (near[...] + near_self[...]).reshape(boxes * 8, 128) * scale + far
 
 
 def in_hbm(x):
@@ -506,16 +513,17 @@
             shape(near_src.shape, jnp.int32),
             shape(trans_src.shape, jnp.int32),
             shape(trans_id.shape, jnp.int32),
-            shape((3 * boxes, 16, 128), BF),
-            shape((3 * boxes, 16, 128), BF),
-            shape((boxes, 128, 16), BF),
+            shape((3 * boxes, 16, 128), F),
+            shape((3 * boxes, 8, 128), F),
+            shape((boxes, 128, 16), F),
+            shape((boxes, 8, 128), F),
             shape((4, 2, 16, 128), BF),
             shape((128, 512), BF),
             shape((8, 512), F),
             shape((8, 512), F),
         ],
         in_specs=[hbm] * 9,
-        out_specs=[vmem] * 10,
+        out_specs=[vmem] * 11,
         scratch_shapes=[
             pltpu.VMEM(cur.shape, BF),
             pltpu.VMEM(pos.shape, BF),
@@ -548,7 +556,7 @@
     field = pl.pallas_call(
         functools.partial(field_kernel, dims),
         out_shape=shape((boxes * waves, width), F),
-        in_specs=[smem] + [vmem] * 9 + [hbm] * 3,
+        in_specs=[smem] + [vmem] * 10 + [hbm] * 3,
         out_specs=vmem,
         scratch_shapes=[
             pltpu.VMEM(radiation.shape, BF),

time: 39.7 us -> 39.5 us (level)
  no operation moved by 1% of the time
where the time goes in v3:
time: 39.5 us; the launch traced here: 39.4 us
  Pallas kernels  38.7 us (98%)
  local copies, waits for them, and re-layouts  0.63 us (2%)
    pallas_call x1, Pallas kernels, per_device(): pl.pallas_call(functools.partial(field_kernel, dims), out_shape=shape((bo...  29.5 us
    pallas_call x1, Pallas kernels, per_device(): pl.pallas_call(functools.partial(prepare_kernel, (n_box, n_dir, boxes, op...  9.17 us

profile of v3, /device:TPU:1, one launch (start us, length us, event | category | flops | bytes accessed | tf_op | source)
XLA Modules:
  0.0 39.4 jit_solution(17964648302131155564)
XLA Ops:
  0.0 9.2 %prepare.1 = (s32[16,27]{1,0:T(8,128)S(1)}, s32[32,32]{1,0:T(8,128)S(1)}, s32[32,32]{1,0:T(8,128)S(1)}, f32[48,16,128]{2,1,0:T(8,128)S(1)}, f32[48,8,128]{2,1,0:...) custom-call(bf16[128,128]{1,0:T(8,128)(2,1)} %bitcast.6, ...), custom_call_target="tpu_custom_call" | custom-call | tf_op jit(solution)/shard_map/prepare/pallas_call | solution.py:510
  9.2 29.5 %field.1 = f32[128,128]{1,0:T(8,128)S(1)} custom-call(s32[16,27]{1,0:T(8,128)S(1)} %get-tuple-element.16.near_list, s32[32,32]{1,0:T(8,128)S(1)} %get-tuple-element.17.src_list, s32[32,32]{1,0:T(8,128)S(1)} %get-tuple-element.18.id_list, f32[48,16,128]{2,1,0:T(8,128)S(1)} %get-tuple-element.19.src_tab, f32[48,8,128]{2,1,0:T(8,128)S(1)} %get-tuple-element.20.x_tab, ...), custom_call_target="tpu_custom_call" | custom-call | tf_op jit(solution)/shard_map/field/pallas_call | solution.py:556
  38.7 0.6 %copy.13 = f32[16,8,128]{2,1,0:T(8,128)} copy(f32[16,8,128]{2,1,0:T(8,128)S(1)} %bitcast.5) | data formatting | bytes 131072

commit v4 on v3

--- a/solution.py
+++ b/solution.py
@@ -24,7 +24,7 @@
 )
 TINY = 2e-6
 
-STRIDE = 4
+STRIDE = 2
 
 
 def cos_turns(turns):
@@ -427,9 +427,9 @@
 
     steps = boxes // STRIDE
     first_half = jnp.logical_and(d >= 2, d < n_dir // 2)
-    gather_at = jnp.where(jnp.logical_and(d >= 2, d < 3 * n_dir // 8), 2, 1)
-    spread_at = jnp.where(first_half, 3, 2)
-    translate_at = jnp.where(first_half, steps, 3)
+    gather_at = jnp.where(d < 2, 1, jnp.where(d < 3 * n_dir // 8, 4, 2))
+    spread_at = jnp.where(first_half, 6, 4)
+    translate_at = jnp.where(first_half, steps, 6)
 
     def boxes_step(step, carry):
         pl.when(step == gather_at)(gather_start)

time: 39.5 us -> 39.8 us (level)
  no operation moved by 1% of the time
where the time goes in v4:
time: 39.8 us; the launch traced here: 39.7 us
  Pallas kernels  39 us (98%)
  local copies, waits for them, and re-layouts  0.63 us (2%)
    pallas_call x1, Pallas kernels, per_device(): pl.pallas_call(functools.partial(field_kernel, dims), out_shape=shape((bo...  29.8 us
    pallas_call x1, Pallas kernels, per_device(): pl.pallas_call(functools.partial(prepare_kernel, (n_box, n_dir, boxes, op...  9.17 us

profile of v4, /device:TPU:1, one launch (start us, length us, event | category | flops | bytes accessed | tf_op | source)
XLA Modules:
  0.0 39.7 jit_solution(5458715794829306940)
XLA Ops:
  0.0 9.2 %prepare.1 = (s32[16,27]{1,0:T(8,128)S(1)}, s32[32,32]{1,0:T(8,128)S(1)}, s32[32,32]{1,0:T(8,128)S(1)}, f32[48,16,128]{2,1,0:T(8,128)S(1)}, f32[48,8,128]{2,1,0:...) custom-call(bf16[128,128]{1,0:T(8,128)(2,1)} %bitcast.6, ...), custom_call_target="tpu_custom_call" | custom-call | tf_op jit(solution)/shard_map/prepare/pallas_call | solution.py:510
  9.2 29.8 %field.1 = f32[128,128]{1,0:T(8,128)S(1)} custom-call(s32[16,27]{1,0:T(8,128)S(1)} %get-tuple-element.16.near_list, s32[32,32]{1,0:T(8,128)S(1)} %get-tuple-element.17.src_list, s32[32,32]{1,0:T(8,128)S(1)} %get-tuple-element.18.id_list, f32[48,16,128]{2,1,0:T(8,128)S(1)} %get-tuple-element.19.src_tab, f32[48,8,128]{2,1,0:T(8,128)S(1)} %get-tuple-element.20.x_tab, ...), custom_call_target="tpu_custom_call" | custom-call | tf_op jit(solution)/shard_map/field/pallas_call | solution.py:556
  39.0 0.6 %copy.13 = f32[16,8,128]{2,1,0:T(8,128)} copy(f32[16,8,128]{2,1,0:T(8,128)S(1)} %bitcast.5) | data formatting | bytes 131072
